TPU v7x, 256 devices: a whole 4x4x8 slice. The times are simulated.
256 devices in a mesh: tile: 64 (over z, y, x_lo), rot: 4 (over x_hi, core).
Axes of the slice: x: 4 (x_hi: 2, x_lo: 2; x = x_hi * 2 + x_lo), y: 4, z: 8, core: 2. Of those that a mesh axis runs over, the one named last changes fastest.
Arguments:
- tomogram: bfloat16 [1024, 128, 128], P('tile'), may hold values from -6 to 6
- templates: bfloat16 [64, 32, 32, 32], P('tile'), may hold values from -6 to 6
- owners: int32 [1], replicated, may hold values from 0 to 63
- orient_ids: int32 [1, 4], P(None, 'rot'), may hold values from 0 to 23
- slice_mask: int32 [1024], P('tile'), may hold values 0 or 1
Outputs:
- best_score: float32 [1024, 128, 128], P('tile')
All inputs are finite; a program needn't handle non-finite values. No bound on the sum of `slice_mask` on one device may be relied on, other than what follows from the above.
Results may differ from a plain program's by a relative error of at most 0.012.
Values may be sent and summed in bfloat16 or wider, within the bound.
No kernel may reach another device: no remote copies, remote signals or barrier semaphores. Data moves between devices by JAX's collectives and lax.ppermute only.
A program may use at most 64 MiB of HBM per device.

v0:
```python
import math

import jax
import jax.numpy as jnp
import numpy as np
from jax import lax
from jax.experimental import pallas as pl
from jax.experimental.pallas import tpu as pltpu
from jax.sharding import Mesh
from jax.sharding import PartitionSpec as P


TILE = ("tile_0", "tile_1", "tile_2")
EDGE = 32
SLAB = 16
WIDE = 128
LENGTH = 48
HALF = LENGTH // 2
FREQS = HALF + 1
PAIRS = (FREQS + 1) // 2
BF16 = jnp.bfloat16
F32 = jnp.float32


def plus(a, b):
    if a is None:
        return b
    return a if b is None else a + b


def minus(a, b):
    if b is None:
        return a
    return -b if a is None else a - b


def weighted(terms):
    total = None
    for value, weight in terms:
        if value is None or abs(weight) < 1e-9:
            continue
        if abs(abs(weight) - 1.0) < 1e-9:
            part = value
        else:
            part = value * jnp.float32(abs(weight))
        if weight > 0:
            total = plus(total, part)
        else:
            total = minus(total, part)
    return total


def cosine(j, k, n):
    return math.cos(2.0 * math.pi * ((j * k) % n) / n)


def sine(j, k, n):
    return math.sin(2.0 * math.pi * ((j * k) % n) / n)


def cos_forward(n, e):
    half = n // 2
    if n % 4:
        return [weighted([(e[j], cosine(j, k, n)) for j in range(half + 1)]) for k in range(half + 1)]
    even = cos_forward(half, e[0::2])
    out = [None] * (half + 1)
    for k in range(n // 4 + 1):
        odd = weighted([(e[j], cosine(j, k, n)) for j in range(1, half, 2)])
        out[k] = plus(even[k], odd)
        if k < n // 4:
            out[half - k] = minus(even[k], odd)
    return out


def sin_forward(n, o):
    half = n // 2
    if n % 4:
        return [weighted([(o[j], sine(j, k, n)) for j in range(1, half)]) if k % half else None for k in range(half + 1)]
    even = sin_forward(half, o[0::2])
    out = [None] * (half + 1)
    for k in range(1, n // 4 + 1):
        odd = weighted([(o[j], sine(j, k, n)) for j in range(1, half, 2)])
        out[k] = plus(even[k], odd) if k < n // 4 else odd
        if k < n // 4:
            out[half - k] = minus(odd, even[k])
    return out


def cos_inverse(n, f, wanted):
    half, quarter = n // 2, n // 4
    if n % 4:
        return {x: weighted([(f[k], cosine(k, x, n)) for k in range(half + 1)]) for x in wanted}
    out = {}
    evens = [x // 2 for x in wanted if x % 2 == 0]
    odds = [x for x in wanted if x % 2]
    if odds:
        q = [minus(f[k], f[half - k]) for k in range(quarter)]
        for x in odds:
            out[x] = weighted([(q[k], cosine(k, x, n)) for k in range(quarter)])
    if evens:
        p = [plus(f[k], f[half - k]) for k in range(quarter)] + [f[quarter]]
        for x, value in cos_inverse(half, p, evens).items():
            out[2 * x] = value
    return out


def sin_inverse(n, g, wanted):
    half, quarter = n // 2, n // 4
    if n % 4:
        return {x: weighted([(g[k], sine(k, x, n)) for k in range(1, half)]) for x in wanted}
    out = {}
    evens = [x // 2 for x in wanted if x % 2 == 0]
    odds = [x for x in wanted if x % 2]
    if odds:
        t = [None] + [plus(g[k], g[half - k]) for k in range(1, quarter)] + [g[quarter]]
        for x in odds:
            out[x] = weighted([(t[k], sine(k, x, n)) for k in range(1, quarter + 1)])
    if evens:
        r = [None] + [minus(g[k], g[half - k]) for k in range(1, quarter)] + [None]
        for x, value in sin_inverse(half, r, evens).items():
            out[2 * x] = value
    return out


def slices_forward(s):
    e = [s[0]] + [plus(s[j], s[LENGTH - j]) for j in range(1, HALF)] + [s[HALF]]
    o = [None] + [minus(s[j], s[LENGTH - j]) for j in range(1, HALF)] + [None]
    return cos_forward(LENGTH, e), sin_forward(LENGTH, o)


def tables():
    def table(rows, cols):
        angle = (np.outer(np.arange(rows), np.arange(cols)) % WIDE).astype(np.float32)
        angle = angle * np.float32(2.0 * math.pi / WIDE)
        return np.cos(angle), np.sin(angle)

    c, s = table(WIDE, WIDE)
    first = np.block([[c, -s], [s, c]])
    second = np.block([[c, s], [-s, c]])
    small_z, small_y = [], []
    for flip in (False, True):
        c, s = table(EDGE, WIDE)
        if flip:
            c, s = c[::-1], s[::-1]
        small_z.append(np.block([[c, -s], [s, c]]))
        small_y.append(np.block([[c.T, s.T], [-s.T, c.T]]))
    return [
        jnp.asarray(t.astype(np.float32)).astype(BF16)
        for t in (first, second, np.stack(small_z), np.stack(small_y))
    ]


def dot(a, b):
    return jnp.dot(a, b, preferred_element_type=F32)


def spot(k):
    return k // 2, (k % 2) * WIDE


def split(value):
    high = value.astype(BF16)
    rest = value - high.astype(F32)
    middle = rest.astype(BF16)
    return high, middle, (rest - middle.astype(F32)).astype(BF16)


def load_rows(tomo_ref, near_ref, far_ref, at):
    s = []
    for ref, count in ((tomo_ref, SLAB), (near_ref, SLAB), (far_ref, SLAB - 1)):
        s += [ref[j, at, :].astype(F32) for j in range(count)]
    return s


def slab_kernel(core_ref, tomo_hbm, own_ref, other_ref, first_ref, second_ref, spec_ref, factor_ref,
                tomo_ref, x_ref, z_ref, sum_ref, square_ref, tomo_sem):
    core = core_ref[0]
    fetch = pltpu.make_async_copy(tomo_hbm, tomo_ref, tomo_sem)
    fetch.start()
    fetch.wait()

    def along_x(near_ref, far_ref):
        def rows(step, carry):
            at = pl.ds(pl.multiple_of(step * 16, 16), 16)
            real, imag = slices_forward(load_rows(tomo_ref, near_ref, far_ref, at) + [None])
            for k in range(FREQS):
                x_ref[k, at, :WIDE] = real[k].astype(BF16)
                if imag[k] is None:
                    x_ref[k, at, WIDE:] = jnp.zeros((16, WIDE), BF16)
                else:
                    x_ref[k, at, WIDE:] = (-imag[k]).astype(BF16)
            return carry

        def windows(step, carry):
            at = pl.ds(pl.multiple_of(step * 16, 16), 16)
            s = load_rows(tomo_ref, near_ref, far_ref, at)
            for target, field in ((sum_ref, s), (square_ref, [value * value for value in s])):
                for reach in (1, 2, 4, 8, 16):
                    field = [field[j] + field[j + reach] for j in range(len(field) - reach)]
                for x in range(SLAB):
                    target[x, at, :] = field[x]
            return carry

        lax.fori_loop(0, WIDE // 16, rows, 0)
        lax.fori_loop(0, WIDE // 16, windows, 0)

    @pl.when(core == 0)
    def _():
        along_x(own_ref, other_ref)

    @pl.when(core != 0)
    def _():
        along_x(other_ref, own_ref)

    for k in range(FREQS):
        pair, lane = spot(k)
        moved = dot(x_ref[k], first_ref[...]).astype(BF16)
        z_ref[pair, :WIDE, lane:lane + WIDE] = moved[:, :WIDE]
        z_ref[pair, WIDE:, lane:lane + WIDE] = moved[:, WIDE:]
    for pair in range(PAIRS):
        width = WIDE if pair == PAIRS - 1 else 2 * WIDE
        spec_ref[pair, :, :width] = dot(second_ref[...], z_ref[pair, :, :width]).astype(BF16)
        if width == WIDE:
            spec_ref[pair, :, WIDE:] = jnp.zeros((2 * WIDE, WIDE), BF16)

    volume = float(EDGE**3)
    ahead = lax.broadcasted_iota(jnp.int32, (WIDE, WIDE), 0) - lax.broadcasted_iota(jnp.int32, (WIDE, WIDE), 1)
    band = (jnp.where(ahead < 0, ahead + WIDE, ahead) < EDGE).astype(F32).astype(BF16)
    band = jnp.concatenate([band] * 3, axis=0)

    def along_y(field):
        for reach in (1, 2, 4, 8, 16):
            field = field + pltpu.roll(field, WIDE - reach, 0)
        return jnp.concatenate(split(field), axis=1)

    def scale(x, carry):
        both = jnp.concatenate([along_y(sum_ref[x]), along_y(square_ref[x])], axis=0)
        box = dot(both, band) / volume
        mean_t, mean_sq = box[:WIDE], box[WIDE:]
        root = lax.rsqrt(mean_sq - mean_t * mean_t + 1e-05) / jnp.float32(math.sqrt(volume))
        factor_ref[x] = root * jnp.float32(2.0 / (LENGTH * WIDE * WIDE))
        return carry

    lax.fori_loop(0, SLAB, scale, 0, unroll=4)


def slab_call(core, tomogram, own, other, first, second):
    vmem = pl.BlockSpec(memory_space=pltpu.VMEM)
    return pl.pallas_call(
        slab_kernel,
        out_shape=(
            jax.ShapeDtypeStruct((PAIRS, 2 * WIDE, 2 * WIDE), BF16),
            jax.ShapeDtypeStruct((SLAB, WIDE, WIDE), F32),
        ),
        in_specs=[pl.BlockSpec(memory_space=pltpu.SMEM), pl.BlockSpec(memory_space=pl.ANY)] + [vmem] * 4,
        out_specs=(vmem, vmem),
        scratch_shapes=[
            pltpu.VMEM((SLAB, WIDE, WIDE), BF16),
            pltpu.VMEM((FREQS, WIDE, 2 * WIDE), BF16),
            pltpu.VMEM((PAIRS, 2 * WIDE, 2 * WIDE), BF16),
            pltpu.VMEM((SLAB, WIDE, WIDE), F32),
            pltpu.VMEM((SLAB, WIDE, WIDE), F32),
            pltpu.SemaphoreType.DMA,
        ],
        compiler_params=pltpu.CompilerParams(vmem_limit_bytes=40 << 20),
        cost_estimate=pl.CostEstimate(flops=4_000_000_000, transcendentals=0, bytes_accessed=6_000_000),
        name="slab",
    )(core, tomogram, own, other, first, second)


def prep_kernel(core_ref, temp_ref, packed_ref):
    values = temp_ref[0].astype(F32).reshape(SLAB * EDGE, EDGE)
    rows = 4 * EDGE
    packed = jnp.concatenate([values[g * rows:(g + 1) * rows] for g in range(4)], axis=1).astype(BF16)
    for member in range(packed_ref.shape[0]):
        packed_ref[member] = packed


def prep_call(core, templates, members):
    return pl.pallas_call(
        prep_kernel,
        out_shape=jax.ShapeDtypeStruct((members, WIDE, WIDE), BF16),
        grid_spec=pltpu.PrefetchScalarGridSpec(
            num_scalar_prefetch=1,
            grid=(1,),
            in_specs=[
                pl.BlockSpec((1, EDGE // 2, EDGE, EDGE), lambda i, core: (0, core[0], 0, 0)),
            ],
            out_specs=pl.BlockSpec((members, WIDE, WIDE), lambda i, core: (0, 0, 0)),
        ),
        name="prep",
    )(core, templates)


def turns_of(index):
    order, flips = lax.div(index, 4), lax.rem(index, 4)
    turn_a = (order == 2) | (order == 3) | (order == 4)
    turn_b = (order == 1) | (order == 2) | (order == 4) | (order == 5)
    turn_c = (order == 1) | (order == 4)
    middle = ((flips == 1) | (flips == 2)).astype(jnp.int32)
    flip_x = jnp.where(order >= 3, 1 - middle, middle)
    return (turn_a, turn_b, turn_c), (flip_x, lax.rem(flips, 2), lax.div(flips, 2))


def swap_last(source, target):
    for a in range(EDGE):
        at = slice(a * EDGE, (a + 1) * EDGE)
        target[at, :] = source[at, :].T


def swap_first(source, target):
    for b in range(EDGE):
        target[b * EDGE:(b + 1) * EDGE, :] = source[pl.ds(b, EDGE, stride=EDGE), :]


def turn(base_ref, cube_ref, spare_ref, turns):
    source = base_ref
    for asked, swap, target in zip(turns, (swap_last, swap_first, swap_last), (cube_ref, spare_ref, cube_ref)):
        def moved(swap=swap, source=source, target=target):
            swap(source, target)

        def kept(source=source, target=target):
            target[...] = source[...]

        pl.when(asked)(moved)
        pl.when(jnp.logical_not(asked))(kept)
        source = target


def match_kernel(core_ref, orient_ref, across_ref, own_ref, other_ref, spec_ref, factor_ref, first_ref, second_ref,
                 small_z_ref, small_y_ref, best_ref,
                 base_ref, cube_ref, spare_ref, packed_ref, a_ref, z_ref, p_ref, q_ref, f_ref):
    core = core_ref[0]
    halves = [ref[...].astype(F32) for ref in (own_ref, other_ref)]
    total = float(EDGE**3)
    center = jnp.sum(halves[0] + halves[1]) / total
    halves = [half - center for half in halves]
    spread = jnp.sum(halves[0] * halves[0] + halves[1] * halves[1]) / total
    root = lax.rsqrt(spread + 1e-05)
    for mine, half in zip((core, 1 - core), halves):
        half = (half * root).astype(BF16).astype(F32)
        for group in range(4):
            start = pl.multiple_of((16 * mine + 4 * group) * EDGE, 128)
            base_ref[pl.ds(start, 4 * EDGE), :] = half[:, group * EDGE:(group + 1) * EDGE]

    flips = []
    for o, index in enumerate((orient_ref[0], across_ref[0])):
        turns, flipped = turns_of(index)
        flips.append(flipped)
        turn(base_ref, cube_ref.at[o], spare_ref.at[o], turns)

    for o in range(2):
        for x in range(EDGE):
            tile = cube_ref[o, x * EDGE:(x + 1) * EDGE, :]
            packed_ref[o, x] = jnp.concatenate([tile[8 * g:8 * g + 8] for g in range(4)], axis=1)

    for o in range(2):
        s = [None] * LENGTH
        for i in range(EDGE):
            s[i + SLAB // 2] = packed_ref[o, jnp.where(flips[o][0] == 1, EDGE - 1 - i, i)]
        real, imag = slices_forward(s)
        for k in range(FREQS):
            share = 0.5 if k in (0, HALF) else 1.0
            for g in range(4):
                at = slice(k * EDGE + 8 * g, k * EDGE + 8 * g + 8)
                lanes = slice(g * EDGE, (g + 1) * EDGE)
                a_ref[o, at, :EDGE] = real[k][:, lanes] * jnp.float32(share)
                if imag[k] is None:
                    a_ref[o, at, EDGE:2 * EDGE] = jnp.zeros((8, EDGE), F32)
                else:
                    a_ref[o, at, EDGE:2 * EDGE] = -imag[k][:, lanes]

    for o in range(2):
        moved = dot(a_ref[o].astype(BF16), small_z_ref[flips[o][2]]).astype(BF16)
        for k in range(FREQS):
            pair, lane = spot(k)
            part = moved[k * EDGE:(k + 1) * EDGE]
            z_ref[o, pair, :EDGE, lane:lane + WIDE] = part[:, :WIDE]
            z_ref[o, pair, EDGE:, lane:lane + WIDE] = part[:, WIDE:]

    for pair in range(PAIRS):
        width = WIDE if pair == PAIRS - 1 else 2 * WIDE
        slab = spec_ref[pair, :, :width].astype(F32)
        slab_r, slab_i = slab[:WIDE], slab[WIDE:]
        for o in range(2):
            temp = dot(small_y_ref[flips[o][1]], z_ref[o, pair, :, :width])
            temp_r, temp_i = temp[:WIDE], temp[WIDE:]
            prod_r = (slab_r * temp_r + slab_i * temp_i).astype(BF16)
            prod_i = (slab_i * temp_r - slab_r * temp_i).astype(BF16)
            for part in range(width // WIDE):
                k = 2 * pair + part
                lanes = slice(part * WIDE, (part + 1) * WIDE)
                p_ref[o, k, :, :WIDE] = prod_r[:, lanes]
                p_ref[o, k, :, WIDE:] = prod_i[:, lanes]

    for o in range(2):
        for k in range(FREQS):
            pair, lane = spot(k)
            moved = dot(p_ref[o, k], second_ref[...]).astype(BF16)
            q_ref[o, pair, :WIDE, lane:lane + WIDE] = moved[:, :WIDE]
            q_ref[o, pair, WIDE:, lane:lane + WIDE] = moved[:, WIDE:]
    for o in range(2):
        for pair in range(PAIRS):
            width = WIDE if pair == PAIRS - 1 else 2 * WIDE
            f_ref[o, pair, :, :width] = dot(first_ref[...], q_ref[o, pair, :, :width])

    def correlation(o, at):
        fr, fi = [], []
        for k in range(FREQS):
            pair, lane = spot(k)
            fr.append(f_ref[o, pair, pl.ds(at, 8), lane:lane + WIDE])
            fi.append(f_ref[o, pair, pl.ds(WIDE + at, 8), lane:lane + WIDE])
        reach = SLAB // 2
        even = cos_inverse(LENGTH, fr, list(range(reach + 1)))
        odd = sin_inverse(LENGTH, fi, list(range(1, reach + 1)))
        values = []
        for lag in range(-reach, SLAB - reach):
            if lag == 0:
                values.append(even[0])
            elif lag > 0:
                values.append(even[lag] - odd[lag])
            else:
                values.append(even[-lag] + odd[-lag])
        return values

    def scores(block, carry):
        at = pl.multiple_of(block * 16, 16)
        rows = []
        for part in (0, 8):
            pair = [correlation(o, at + part) for o in range(2)]
            rows.append([jnp.maximum(one, two) for one, two in zip(*pair)])
        for x in range(SLAB):
            value = jnp.concatenate([rows[0][x], rows[1][x]], axis=0) * factor_ref[x, pl.ds(at, 16), :]
            best_ref[x, pl.ds(at, 16), :] = value.astype(BF16)
        return carry

    lax.fori_loop(0, WIDE // 16, scores, 0)


def match_call(core, orient, across, own, other, spec, factor, first, second, small_z, small_y):
    vmem = pl.BlockSpec(memory_space=pltpu.VMEM)
    smem = pl.BlockSpec(memory_space=pltpu.SMEM)
    cube = EDGE * EDGE
    return pl.pallas_call(
        match_kernel,
        out_shape=jax.ShapeDtypeStruct((SLAB, WIDE, WIDE), BF16),
        in_specs=[smem] * 3 + [vmem] * 8,
        out_specs=vmem,
        scratch_shapes=[
            pltpu.VMEM((cube, EDGE), F32),
            pltpu.VMEM((2, cube, EDGE), F32),
            pltpu.VMEM((2, cube, EDGE), F32),
            pltpu.VMEM((2, EDGE, 8, WIDE), F32),
            pltpu.VMEM((2, FREQS * EDGE, 2 * EDGE), F32),
            pltpu.VMEM((2, PAIRS, 2 * EDGE, 2 * WIDE), BF16),
            pltpu.VMEM((2, FREQS, WIDE, 2 * WIDE), BF16),
            pltpu.VMEM((2, PAIRS, 2 * WIDE, 2 * WIDE), BF16),
            pltpu.VMEM((2, PAIRS, 2 * WIDE, 2 * WIDE), F32),
        ],
        compiler_params=pltpu.CompilerParams(vmem_limit_bytes=40 << 20),
        cost_estimate=pl.CostEstimate(flops=8_000_000_000, transcendentals=0, bytes_accessed=6_000_000),
        name="match",
    )(core, orient, across, own, other, spec, factor, first, second, small_z, small_y)


def swapped(value, axis):
    return lax.ppermute(value, axis, [(0, 1), (1, 0)])


def from_member(value, axis, root):
    sent = jnp.broadcast_to(value[None], (lax.axis_size(axis), *value.shape))
    got = lax.all_to_all(sent, axis, 0, 0, tiled=True)
    return lax.dynamic_index_in_dim(got, root, 0, keepdims=False)


def halo_pairs(tiles):
    return [
        (2 * tile + core, 2 * (tile - 1 - core) + core)
        for tile in range(tiles)
        for core in range(2)
        if tile - 1 - core >= 0
    ]


def shards(tomogram, templates, owners, orient_ids, slice_mask):
    core_arg = lax.axis_index("core").astype(jnp.int32)[None]
    first, second, small_z, small_y = tables()
    columns = lax.axis_size("tile_2")
    depth, plane = lax.axis_size("tile_0"), lax.axis_size("tile_1") * columns
    root_plane, root_z = lax.rem(owners[0], plane), lax.div(owners[0], plane)

    sent = prep_call(core_arg, templates, plane)
    got = lax.all_to_all(sent, ("tile_1", "tile_2"), 0, 0, tiled=True)
    half = lax.dynamic_index_in_dim(got, root_plane, 0, keepdims=False)

    halo = lax.ppermute(tomogram, TILE + ("core",), halo_pairs(depth * plane))
    across = swapped(orient_ids[0], "far")
    other_halo = swapped(halo, "core")

    half = from_member(half, "tile_0", root_z)
    other_half = swapped(half, "core")

    spec, factor = slab_call(core_arg, tomogram, halo, other_halo, first, second)

    best = match_call(core_arg, orient_ids[0], across, half, other_half, spec, factor, first, second, small_z, small_y)
    best = jnp.maximum(best, swapped(best, "core"))
    return best.astype(F32) * slice_mask.astype(F32)[:, None, None]


def solution(mesh):
    torus = Mesh(
        mesh.devices.reshape(8, 4, 2, 2, 2), ("tile_0", "tile_1", "tile_2", "far", "core")
    )
    in_specs = (P(TILE, None, None), P(TILE, None, None, None), P(), P(None, ("far", "core")), P(TILE))
    out_specs = P(TILE, None, None)
    return jax.shard_map(
        shards, mesh=torus, in_specs=in_specs, out_specs=out_specs, check_vma=False
    )
```

profile of v0, /device:TPU:1, one launch (start us, length us, event | category | flops | bytes accessed | tf_op | source)
XLA Modules:
  0.0 61.1 jit_solution(8225789358852656173)
XLA Ops:
  0.0 0.0 copy-start.1
  0.0 0.0 copy-start.2
  0.0 0.0 copy-start
  0.0 1.4 %collective-permute-start.2 = (bf16[16,128,128]{2,1,0:T(8,128)(2,1)}, bf16[16,128,128]{2,1,0:T(8,128)(2,1)S(1)}, u32[]{:S(2)}, u32[]{:S(2)}) collective-permute-start(bf16[16,128,128]{2,1,0:T(8,128)(2,1)} %tomo_hbm.1), channel_id=1, source_target_pairs={{4,0},{8,4},{9,1},{12,8},{13,5},{16,12},{17,9},{20,16},{21,13},{24... | collective-permute-start | bytes 1572872 | tf_op jit(solution)/shard_map/ppermute | solution.py:496
  1.4 1.7 %prep.1 = bf16[8,128,128]{2,1,0:T(8,128)(2,1)} custom-call(s32[1]{0:T(128)} %bitcast.core_ref, bf16[1,32,32,32]{3,2,1,0:T(8,128)(2,1)} %temp_ref.1), custom_call_target="tpu_custom_call" | custom-call | tf_op jit(solution)/shard_map/prep/pallas_call | solution.py:280
  3.2 6.8 %all-to-all-start = ((bf16[8,128,128]{2,1,0:T(8,128)(2,1)}), bf16[8,128,128]{2,1,0:T(8,128)(2,1)S(1)}, u32[]{:S(2)}, u32[]{:S(2)}) async-start(bf16[8,128,128]{2,1,0:T(8,128)(2,1)} %prep.1), calls=%async_computation | async-start | bytes 524288 | tf_op jit(solution)/shard_map/all_to_all | solution.py:493
  10.7 10.9 %all-to-all-done = bf16[8,128,128]{2,1,0:T(8,128)(2,1)S(1)} async-done(((bf16[8,128,128]{2,1,0:T(8,128)(2,1)}), bf16[8,128,128]{2,1,0:T(8,128)(2,1)S(1)}, u32[]{:S(2)}, u32[]{:S(2)}) %all-to-all-start) | async-done | bytes 262176 | tf_op jit(solution)/shard_map/all_to_all | solution.py:493
  21.5 0.7 %broadcast_in_dim.14 = bf16[8,128,128]{2,1,0:T(8,128)(2,1)} broadcast(bf16[128,128]{1,0:T(8,128)(2,1)S(1)} %dynamic-slice_bitcast_fusion.1), dimensions={1,2} | broadcast | bytes 294912 | tf_op jit(solution)/shard_map/broadcast_in_dim | solution.py:471
  22.3 8.5 %all-to-all-start.1 = ((bf16[8,128,128]{2,1,0:T(8,128)(2,1)}), bf16[8,128,128]{2,1,0:T(8,128)(2,1)S(1)}, u32[]{:S(2)}, u32[]{:S(2)}) async-start(bf16[8,128,128]{2,1,0:T(8,128)(2,1)} %broadcast_in_dim.14), calls=%async_computation.1 | async-start | bytes 524288 | tf_op jit(solution)/shard_map/all_to_all | solution.py:472
  30.8 0.0 collective-permute-done.2.own_ref
  30.8 1.1 %collective-permute-start.3 = (bf16[16,128,128]{2,1,0:T(8,128)(2,1)S(1)}, bf16[16,128,128]{2,1,0:T(8,128)(2,1)S(1)}, u32[]{:S(2)}, u32[]{:S(2)}) collective-permute-start(bf16[16,128,128]{2,1,0:T(8,128)(2,1)S(1)} %collective-permute-done.2.own_ref), channel_id=1, source_target_pairs={{0,1},{1,0},{2,3},{3,2},{4,5},{5,4},{6,7},{7,6},{8,9},{9,8},{10,11... | collective-permute-start | bytes 1572872 | tf_op jit(solution)/shard_map/ppermute | solution.py:467
  31.8 3.0 %collective-permute-start = (s32[1]{0:T(128)}, s32[1]{0:T(128)}, u32[]{:S(2)}, u32[]{:S(2)}) collective-permute-start(s32[1]{0:T(128)} %bitcast.1), channel_id=1, source_target_pairs={{0,2},{2,0},{1,3},{3,1},{4,6},{6,4},{5,7},{7,5},{8,10},{10,8},{9,1... | collective-permute-start | bytes 20 | tf_op jit(solution)/shard_map/ppermute | solution.py:467
  35.5 5.7 %all-to-all-done.1 = bf16[8,128,128]{2,1,0:T(8,128)(2,1)S(1)} async-done(((bf16[8,128,128]{2,1,0:T(8,128)(2,1)}), bf16[8,128,128]{2,1,0:T(8,128)(2,1)S(1)}, u32[]{:S(2)}, u32[]{:S(2)}) %all-to-all-start.1) | async-done | bytes 262176 | tf_op jit(solution)/shard_map/all_to_all | solution.py:472
  41.2 0.0 copy-start.3
  41.2 0.0 copy-start.4
  41.2 2.5 %collective-permute-start.1 = (bf16[128,128]{1,0:T(8,128)(2,1)S(1)}, bf16[128,128]{1,0:T(8,128)(2,1)S(1)}, u32[]{:S(2)}, u32[]{:S(2)}) collective-permute-start(bf16[128,128]{1,0:T(8,128)(2,1)S(1)} %dynamic-slice_bitcast_fusion.own_ref), channel_id=1, source_target_pairs={{0,1},{1,0},{2,3},{3,2},{4,5},{5,4},{6,7},{7,6},{8,9},{9,8},{10,11... | collective-permute-start | bytes 98312 | tf_op jit(solution)/shard_map/ppermute | solution.py:467
  43.7 0.0 collective-permute-done.3.other_ref
  43.7 0.0 copy-done.1
  43.7 0.0 copy-done.2
  43.7 0.0 copy-done
  43.7 6.5 %slab.1 = (bf16[13,256,256]{2,1,0:T(8,128)(2,1)S(1)}, f32[16,128,128]{2,1,0:T(8,128)S(1)}) custom-call(s32[1]{0:T(128)} %bitcast.core_ref, bf16[16,128,128]{2,1,0:T(8,128)(2,1)S(1)} %copy-done, bf16[16,128,128]{2,1,0:T(8,128)(2,1)S(1)} %collective-permute-done.2.own_ref, bf16[16,128,128]{2,1,0:T(8,128)(2,1)S(1)} %collective-permute-done.3.other_ref, ...), custom_call_target="tpu_custom_call" | custom-call | flops 4000000000 | bytes 6000000 | tf_op jit(solution)/shard_map/slab/pallas_call | solution.py:249
  50.2 0.0 collective-permute-done.across_ref
  50.2 0.0 collective-permute-done.1.other_ref
  50.2 0.0 copy-done.3
  50.2 0.0 copy-done.4
  50.2 0.0 copy-start.5
  50.3 7.7 %match.1 = bf16[16,128,128]{2,1,0:T(8,128)(2,1)S(1)} custom-call(s32[1]{0:T(128)} %bitcast.core_ref, s32[1]{0:T(128)} %bitcast.10.orient_ref, s32[1]{0:T(128)} %collective-permute-done.across_ref, bf16[128,128]{1,0:T(8,128)(2,1)S(1)} %dynamic-slice_bitcast_fusion.own_ref, bf16[128,128]{1,0:T(8,128)(2,1)S(1)} %collective-permute-done.1.other_ref, ...), custom_call_target="tpu_custom_call" | custom-call | flops 8000000000 | bytes 6000000 | tf_op jit(solution)/shard_map/match/pallas_call | solution.py:444
  58.0 0.1 collective-permute-start.4
  58.1 0.0 copy-done.5
  58.1 1.9 %collective-permute-done.4 = bf16[16,128,128]{2,1,0:T(8,128)(2,1)S(1)} collective-permute-done((bf16[16,128,128]{2,1,0:T(8,128)(2,1)S(1)}, bf16[16,128,128]{2,1,0:T(8,128)(2,1)S(1)}, u32[]{:S(2)}, u32[]{:S(2)}) %collective-permute-start.4) | collective-permute-done | bytes 524320 | tf_op jit(solution)/shard_map/ppermute | solution.py:467
  60.0 1.1 %convert_multiply_fusion = f32[16,128,128]{2,1,0:T(8,128)} fusion(f32[16]{0:T(128)S(1)} %convert_element_type.23, bf16[16,128,128]{2,1,0:T(8,128)(2,1)S(1)} %match.1, bf16[16,128,128]{2,1,0:T(8,128)(2,1)S(1)} %collective-permute-done.4), kind=kLoop, calls=%fused_computation | loop fusion | flops 786432 | bytes 2097216 | tf_op jit(solution)/shard_map/mul | solution.py:507
  (3 shorter events, 0.0 us)
Async XLA Ops:
  0.0 43.7 %copy-start.1 = (bf16[256,256]{1,0:T(8,128)(2,1)S(1)}, bf16[256,256]{1,0:T(8,128)(2,1)}, u32[]{:S(2)}) copy-start(bf16[256,256]{1,0:T(8,128)(2,1)} %constant.35.first_ref) | copy-start | bytes 393220
  0.0 43.7 %copy-start.2 = (bf16[256,256]{1,0:T(8,128)(2,1)S(1)}, bf16[256,256]{1,0:T(8,128)(2,1)}, u32[]{:S(2)}) copy-start(bf16[256,256]{1,0:T(8,128)(2,1)} %constant.36.second_ref) | copy-start | bytes 393220
  0.0 43.7 %copy-start = (bf16[16,128,128]{2,1,0:T(8,128)(2,1)S(1)}, bf16[16,128,128]{2,1,0:T(8,128)(2,1)}, u32[]{:S(2)}) copy-start(bf16[16,128,128]{2,1,0:T(8,128)(2,1)} %tomo_hbm.1) | copy-start | bytes 1572868
  0.0 30.8 %collective-permute-start.2 = (bf16[16,128,128]{2,1,0:T(8,128)(2,1)}, bf16[16,128,128]{2,1,0:T(8,128)(2,1)S(1)}, u32[]{:S(2)}, u32[]{:S(2)}) collective-permute-start(bf16[16,128,128]{2,1,0:T(8,128)(2,1)} %tomo_hbm.1), channel_id=1, source_target_pairs={{4,0},{8,4},{9,1},{12,8},{13,5},{16,12},{17,9},{20,16},{21,13},{24... | collective-permute-start | bytes 1572872 | tf_op jit(solution)/shard_map/ppermute | solution.py:496
  3.2 18.4 %all-to-all-start = ((bf16[8,128,128]{2,1,0:T(8,128)(2,1)}), bf16[8,128,128]{2,1,0:T(8,128)(2,1)S(1)}, u32[]{:S(2)}, u32[]{:S(2)}) async-start(bf16[8,128,128]{2,1,0:T(8,128)(2,1)} %prep.1), calls=%async_computation | async-start | bytes 524288 | tf_op jit(solution)/shard_map/all_to_all | solution.py:493
  22.3 18.9 %all-to-all-start.1 = ((bf16[8,128,128]{2,1,0:T(8,128)(2,1)}), bf16[8,128,128]{2,1,0:T(8,128)(2,1)S(1)}, u32[]{:S(2)}, u32[]{:S(2)}) async-start(bf16[8,128,128]{2,1,0:T(8,128)(2,1)} %broadcast_in_dim.14), calls=%async_computation.1 | async-start | bytes 524288 | tf_op jit(solution)/shard_map/all_to_all | solution.py:472
  30.8 12.9 %collective-permute-start.3 = (bf16[16,128,128]{2,1,0:T(8,128)(2,1)S(1)}, bf16[16,128,128]{2,1,0:T(8,128)(2,1)S(1)}, u32[]{:S(2)}, u32[]{:S(2)}) collective-permute-start(bf16[16,128,128]{2,1,0:T(8,128)(2,1)S(1)} %collective-permute-done.2.own_ref), channel_id=1, source_target_pairs={{0,1},{1,0},{2,3},{3,2},{4,5},{5,4},{6,7},{7,6},{8,9},{9,8},{10,11... | collective-permute-start | bytes 1572872 | tf_op jit(solution)/shard_map/ppermute | solution.py:467
  31.8 18.4 %collective-permute-start = (s32[1]{0:T(128)}, s32[1]{0:T(128)}, u32[]{:S(2)}, u32[]{:S(2)}) collective-permute-start(s32[1]{0:T(128)} %bitcast.1), channel_id=1, source_target_pairs={{0,2},{2,0},{1,3},{3,1},{4,6},{6,4},{5,7},{7,5},{8,10},{10,8},{9,1... | collective-permute-start | bytes 20 | tf_op jit(solution)/shard_map/ppermute | solution.py:467
  41.2 9.0 %copy-start.3 = (bf16[2,256,64]{2,1,0:T(8,128)(2,1)S(1)}, bf16[2,256,64]{2,1,0:T(8,128)(2,1)}, u32[]{:S(2)}) copy-start(bf16[2,256,64]{2,1,0:T(8,128)(2,1)} %constant.38.small_y_ref) | copy-start | bytes 196612
  41.2 9.0 %copy-start.4 = (bf16[2,64,256]{2,1,0:T(8,128)(2,1)S(1)}, bf16[2,64,256]{2,1,0:T(8,128)(2,1)}, u32[]{:S(2)}) copy-start(bf16[2,64,256]{2,1,0:T(8,128)(2,1)} %constant.37.small_z_ref) | copy-start | bytes 196612
  41.2 9.0 %collective-permute-start.1 = (bf16[128,128]{1,0:T(8,128)(2,1)S(1)}, bf16[128,128]{1,0:T(8,128)(2,1)S(1)}, u32[]{:S(2)}, u32[]{:S(2)}) collective-permute-start(bf16[128,128]{1,0:T(8,128)(2,1)S(1)} %dynamic-slice_bitcast_fusion.own_ref), channel_id=1, source_target_pairs={{0,1},{1,0},{2,3},{3,2},{4,5},{5,4},{6,7},{7,6},{8,9},{9,8},{10,11... | collective-permute-start | bytes 98312 | tf_op jit(solution)/shard_map/ppermute | solution.py:467
  50.2 7.8 %copy-start.5 = (s32[16]{0:T(128)S(1)}, s32[16]{0:T(128)}, u32[]{:S(2)}) copy-start(s32[16]{0:T(128)} %param.13) | copy-start | bytes 196
  58.0 2.0 %collective-permute-start.4 = (bf16[16,128,128]{2,1,0:T(8,128)(2,1)S(1)}, bf16[16,128,128]{2,1,0:T(8,128)(2,1)S(1)}, u32[]{:S(2)}, u32[]{:S(2)}) collective-permute-start(bf16[16,128,128]{2,1,0:T(8,128)(2,1)S(1)} %match.1), channel_id=1, source_target_pairs={{0,1},{1,0},{2,3},{3,2},{4,5},{5,4},{6,7},{7,6},{8,9},{9,8},{10,11... | collective-permute-start | bytes 1572872 | tf_op jit(solution)/shard_map/ppermute | solution.py:467
where the time goes:
time: 62 us; the launch traced here: 61.1 us
  starting transfers between devices  23.4 us (38%)
  waiting for transfers between devices  18.4 us (30%)
  Pallas kernels  15.9 us (26%)
  between operations  1.47 us (2%)
  other arithmetic  1.14 us (2%)
  local copies, waits for them, and re-layouts  0.77 us (1%)
    all_to_all x1, waiting for transfers between devices, shards(): got = lax.all_to_all(sent, ('tile_1', 'tile_2'), 0, 0, tiled=True)  10.9 us
    all_to_all x1, starting transfers between devices, from_member(): got = lax.all_to_all(sent, axis, 0, 0, tiled=True)  8.49 us
    pallas_call x1, Pallas kernels, match_call(): pl.pallas_call(match_kernel, out_shape=jax.ShapeDtypeStruct((SLAB, WIDE,...  7.71 us
    all_to_all x1, starting transfers between devices, shards(): got = lax.all_to_all(sent, ('tile_1', 'tile_2'), 0, 0, tiled=True)  6.83 us
    ppermute x4, starting transfers between devices, swapped(): return lax.ppermute(value, axis, [(0, 1), (1, 0)])  6.64 us
    pallas_call x1, Pallas kernels, slab_call(): pl.pallas_call(slab_kernel, out_shape=(jax.ShapeDtypeStruct((PAIRS, 2 * W...  6.47 us
    all_to_all x1, waiting for transfers between devices, from_member(): got = lax.all_to_all(sent, axis, 0, 0, tiled=True)  5.68 us
    ppermute x4, waiting for transfers between devices, swapped(): return lax.ppermute(value, axis, [(0, 1), (1, 0)])  1.88 us
  transfers between devices with their start and end apart: 7, of which 3 were waited for; matrix products, arithmetic and copies ran while one was open for 1% of the time, Pallas kernels for 13%

commit v1 on v0

--- a/solution.py
+++ b/solution.py
@@ -172,13 +172,57 @@
     return s
 
 
-def slab_kernel(core_ref, tomo_hbm, own_ref, other_ref, first_ref, second_ref, spec_ref, factor_ref,
-                tomo_ref, x_ref, z_ref, sum_ref, square_ref, tomo_sem):
-    core = core_ref[0]
+def either(core, one, two, run):
+    @pl.when(core == 0)
+    def _():
+        run(one, two)
+
+    @pl.when(core != 0)
+    def _():
+        run(two, one)
+
+
+def factor_kernel(core_ref, tomo_hbm, own_ref, other_ref, factor_ref, tomo_ref, sum_ref, square_ref, tomo_sem):
     fetch = pltpu.make_async_copy(tomo_hbm, tomo_ref, tomo_sem)
     fetch.start()
+    volume = float(EDGE**3)
+    ahead = lax.broadcasted_iota(jnp.int32, (WIDE, WIDE), 0) - lax.broadcasted_iota(jnp.int32, (WIDE, WIDE), 1)
+    band = (jnp.where(ahead < 0, ahead + WIDE, ahead) < EDGE).astype(F32).astype(BF16)
+    band = jnp.concatenate([band] * 3, axis=0)
     fetch.wait()
 
+    def along_x(near_ref, far_ref):
+        def windows(step, carry):
+            at = pl.ds(pl.multiple_of(step * 16, 16), 16)
+            s = load_rows(tomo_ref, near_ref, far_ref, at)
+            for target, field in ((sum_ref, s), (square_ref, [value * value for value in s])):
+                for reach in (1, 2, 4, 8, 16):
+                    field = [field[j] + field[j + reach] for j in range(len(field) - reach)]
+                for x in range(SLAB):
+                    target[x, at, :] = field[x]
+            return carry
+
+        lax.fori_loop(0, WIDE // 16, windows, 0)
+
+    either(core_ref[0], own_ref, other_ref, along_x)
+
+    def along_y(field):
+        for reach in (1, 2, 4, 8, 16):
+            field = field + pltpu.roll(field, WIDE - reach, 0)
+        return jnp.concatenate(split(field), axis=1)
+
+    def scale(x, carry):
+        both = jnp.concatenate([along_y(sum_ref[x]), along_y(square_ref[x])], axis=0)
+        box = dot(both, band) / volume
+        mean_t, mean_sq = box[:WIDE], box[WIDE:]
+        root = lax.rsqrt(mean_sq - mean_t * mean_t + 1e-05) / jnp.float32(math.sqrt(volume))
+        factor_ref[x] = root * jnp.float32(2.0 / (LENGTH * WIDE * WIDE))
+        return carry
+
+    lax.fori_loop(0, SLAB, scale, 0, unroll=4)
+
+
+def spectrum_kernel(core_ref, tomo_ref, own_ref, other_ref, first_ref, second_ref, spec_ref, x_ref, z_ref):
     def along_x(near_ref, far_ref):
         def rows(step, carry):
             at = pl.ds(pl.multiple_of(step * 16, 16), 16)
@@ -191,26 +235,9 @@
                     x_ref[k, at, WIDE:] = (-imag[k]).astype(BF16)
             return carry
 
-        def windows(step, carry):
-            at = pl.ds(pl.multiple_of(step * 16, 16), 16)
-            s = load_rows(tomo_ref, near_ref, far_ref, at)
-            for target, field in ((sum_ref, s), (square_ref, [value * value for value in s])):
-                for reach in (1, 2, 4, 8, 16):
-                    field = [field[j] + field[j + reach] for j in range(len(field) - reach)]
-                for x in range(SLAB):
-                    target[x, at, :] = field[x]
-            return carry
-
         lax.fori_loop(0, WIDE // 16, rows, 0)
-        lax.fori_loop(0, WIDE // 16, windows, 0)
-
-    @pl.when(core == 0)
-    def _():
-        along_x(own_ref, other_ref)
-
-    @pl.when(core != 0)
-    def _():
-        along_x(other_ref, own_ref)
+
+    either(core_ref[0], own_ref, other_ref, along_x)
 
     for k in range(FREQS):
         pair, lane = spot(k)
@@ -223,48 +250,42 @@
         if width == WIDE:
             spec_ref[pair, :, WIDE:] = jnp.zeros((2 * WIDE, WIDE), BF16)
 
-    volume = float(EDGE**3)
-    ahead = lax.broadcasted_iota(jnp.int32, (WIDE, WIDE), 0) - lax.broadcasted_iota(jnp.int32, (WIDE, WIDE), 1)
-    band = (jnp.where(ahead < 0, ahead + WIDE, ahead) < EDGE).astype(F32).astype(BF16)
-    band = jnp.concatenate([band] * 3, axis=0)
-
-    def along_y(field):
-        for reach in (1, 2, 4, 8, 16):
-            field = field + pltpu.roll(field, WIDE - reach, 0)
-        return jnp.concatenate(split(field), axis=1)
-
-    def scale(x, carry):
-        both = jnp.concatenate([along_y(sum_ref[x]), along_y(square_ref[x])], axis=0)
-        box = dot(both, band) / volume
-        mean_t, mean_sq = box[:WIDE], box[WIDE:]
-        root = lax.rsqrt(mean_sq - mean_t * mean_t + 1e-05) / jnp.float32(math.sqrt(volume))
-        factor_ref[x] = root * jnp.float32(2.0 / (LENGTH * WIDE * WIDE))
-        return carry
-
-    lax.fori_loop(0, SLAB, scale, 0, unroll=4)
-
-
-def slab_call(core, tomogram, own, other, first, second):
+
+def factor_call(core, tomogram, own, other):
     vmem = pl.BlockSpec(memory_space=pltpu.VMEM)
     return pl.pallas_call(
-        slab_kernel,
+        factor_kernel,
         out_shape=(
-            jax.ShapeDtypeStruct((PAIRS, 2 * WIDE, 2 * WIDE), BF16),
             jax.ShapeDtypeStruct((SLAB, WIDE, WIDE), F32),
+            jax.ShapeDtypeStruct((SLAB, WIDE, WIDE), BF16),
         ),
-        in_specs=[pl.BlockSpec(memory_space=pltpu.SMEM), pl.BlockSpec(memory_space=pl.ANY)] + [vmem] * 4,
+        in_specs=[pl.BlockSpec(memory_space=pltpu.SMEM), pl.BlockSpec(memory_space=pl.ANY), vmem, vmem],
         out_specs=(vmem, vmem),
         scratch_shapes=[
-            pltpu.VMEM((SLAB, WIDE, WIDE), BF16),
-            pltpu.VMEM((FREQS, WIDE, 2 * WIDE), BF16),
-            pltpu.VMEM((PAIRS, 2 * WIDE, 2 * WIDE), BF16),
             pltpu.VMEM((SLAB, WIDE, WIDE), F32),
             pltpu.VMEM((SLAB, WIDE, WIDE), F32),
             pltpu.SemaphoreType.DMA,
         ],
-        compiler_params=pltpu.CompilerParams(vmem_limit_bytes=40 << 20),
+        compiler_params=pltpu.CompilerParams(vmem_limit_bytes=8 << 20),
         cost_estimate=pl.CostEstimate(flops=4_000_000_000, transcendentals=0, bytes_accessed=6_000_000),
-        name="slab",
+        name="factor",
+    )(core, tomogram, own, other)
+
+
+def spectrum_call(core, tomogram, own, other, first, second):
+    vmem = pl.BlockSpec(memory_space=pltpu.VMEM)
+    return pl.pallas_call(
+        spectrum_kernel,
+        out_shape=jax.ShapeDtypeStruct((PAIRS, 2 * WIDE, 2 * WIDE), BF16),
+        in_specs=[pl.BlockSpec(memory_space=pltpu.SMEM)] + [vmem] * 5,
+        out_specs=vmem,
+        scratch_shapes=[
+            pltpu.VMEM((FREQS, WIDE, 2 * WIDE), BF16),
+            pltpu.VMEM((PAIRS, 2 * WIDE, 2 * WIDE), BF16),
+        ],
+        compiler_params=pltpu.CompilerParams(vmem_limit_bytes=10 << 20),
+        cost_estimate=pl.CostEstimate(flops=4_000_000_000, transcendentals=0, bytes_accessed=6_000_000),
+        name="spectrum",
     )(core, tomogram, own, other, first, second)
 
 
@@ -457,7 +478,7 @@
             pltpu.VMEM((2, PAIRS, 2 * WIDE, 2 * WIDE), BF16),
             pltpu.VMEM((2, PAIRS, 2 * WIDE, 2 * WIDE), F32),
         ],
-        compiler_params=pltpu.CompilerParams(vmem_limit_bytes=40 << 20),
+        compiler_params=pltpu.CompilerParams(vmem_limit_bytes=24 << 20),
         cost_estimate=pl.CostEstimate(flops=8_000_000_000, transcendentals=0, bytes_accessed=6_000_000),
         name="match",
     )(core, orient, across, own, other, spec, factor, first, second, small_z, small_y)
@@ -500,7 +521,8 @@
     half = from_member(half, "tile_0", root_z)
     other_half = swapped(half, "core")
 
-    spec, factor = slab_call(core_arg, tomogram, halo, other_halo, first, second)
+    factor, staged = factor_call(core_arg, tomogram, halo, other_halo)
+    spec = spectrum_call(core_arg, staged, halo, other_halo, first, second)
 
     best = match_call(core_arg, orient_ids[0], across, half, other_half, spec, factor, first, second, small_z, small_y)
     best = jnp.maximum(best, swapped(best, "core"))

time: 62 us -> 62.1 us (level)
    pallas_call x1 -> x2, Pallas kernels: 6.47 us -> 6.52 us  [the longest x1 3.3 us: spectrum_call(): pl.pallas_call(spectrum_kernel, out_shape=jax.ShapeDtypeStruct((PAIRS, 2...]
where the time goes in v1:
time: 62.1 us; the launch traced here: 61.2 us
  starting transfers between devices  23.4 us (38%)
  waiting for transfers between devices  18.4 us (30%)
  Pallas kernels  15.9 us (26%)
  between operations  1.49 us (2%)
  other arithmetic  1.14 us (2%)
  local copies, waits for them, and re-layouts  0.78 us (1%)
    all_to_all x1, waiting for transfers between devices, shards(): got = lax.all_to_all(sent, ('tile_1', 'tile_2'), 0, 0, tiled=True)  10.9 us
    all_to_all x1, starting transfers between devices, from_member(): got = lax.all_to_all(sent, axis, 0, 0, tiled=True)  8.49 us
    pallas_call x1, Pallas kernels, match_call(): pl.pallas_call(match_kernel, out_shape=jax.ShapeDtypeStruct((SLAB, WIDE,...  7.7 us
    all_to_all x1, starting transfers between devices, shards(): got = lax.all_to_all(sent, ('tile_1', 'tile_2'), 0, 0, tiled=True)  6.83 us
    ppermute x4, starting transfers between devices, swapped(): return lax.ppermute(value, axis, [(0, 1), (1, 0)])  6.64 us
    all_to_all x1, waiting for transfers between devices, from_member(): got = lax.all_to_all(sent, axis, 0, 0, tiled=True)  5.68 us
    pallas_call x1, Pallas kernels, spectrum_call(): pl.pallas_call(spectrum_kernel, out_shape=jax.ShapeDtypeStruct((PAIRS, 2...  3.3 us
    pallas_call x1, Pallas kernels, factor_call(): pl.pallas_call(factor_kernel, out_shape=(jax.ShapeDtypeStruct((SLAB, WIDE...  3.22 us
  transfers between devices with their start and end apart: 7, of which 3 were waited for; matrix products, arithmetic and copies ran while one was open for 1% of the time, Pallas kernels for 13%

profile of v1, /device:TPU:1, one launch (start us, length us, event | category | flops | bytes accessed | tf_op | source)
XLA Modules:
  0.0 61.2 jit_solution(7952047808207578502)
XLA Ops:
  0.0 0.0 copy-start
  0.0 1.4 %collective-permute-start.2 = (bf16[16,128,128]{2,1,0:T(8,128)(2,1)}, bf16[16,128,128]{2,1,0:T(8,128)(2,1)S(1)}, u32[]{:S(2)}, u32[]{:S(2)}) collective-permute-start(bf16[16,128,128]{2,1,0:T(8,128)(2,1)} %tomo_hbm.1), channel_id=1, source_target_pairs={{4,0},{8,4},{9,1},{12,8},{13,5},{16,12},{17,9},{20,16},{21,13},{24... | collective-permute-start | bytes 1572872 | tf_op jit(solution)/shard_map/ppermute | solution.py:517
  1.4 1.7 %prep.1 = bf16[8,128,128]{2,1,0:T(8,128)(2,1)} custom-call(s32[1]{0:T(128)} %bitcast.core_ref, bf16[1,32,32,32]{3,2,1,0:T(8,128)(2,1)} %temp_ref.1), custom_call_target="tpu_custom_call" | custom-call | tf_op jit(solution)/shard_map/prep/pallas_call | solution.py:301
  3.1 6.8 %all-to-all-start = ((bf16[8,128,128]{2,1,0:T(8,128)(2,1)}), bf16[8,128,128]{2,1,0:T(8,128)(2,1)S(1)}, u32[]{:S(2)}, u32[]{:S(2)}) async-start(bf16[8,128,128]{2,1,0:T(8,128)(2,1)} %prep.1), calls=%async_computation | async-start | bytes 524288 | tf_op jit(solution)/shard_map/all_to_all | solution.py:514
  10.6 10.9 %all-to-all-done = bf16[8,128,128]{2,1,0:T(8,128)(2,1)S(1)} async-done(((bf16[8,128,128]{2,1,0:T(8,128)(2,1)}), bf16[8,128,128]{2,1,0:T(8,128)(2,1)S(1)}, u32[]{:S(2)}, u32[]{:S(2)}) %all-to-all-start) | async-done | bytes 262176 | tf_op jit(solution)/shard_map/all_to_all | solution.py:514
  21.5 0.7 %broadcast_in_dim.14 = bf16[8,128,128]{2,1,0:T(8,128)(2,1)} broadcast(bf16[128,128]{1,0:T(8,128)(2,1)S(1)} %dynamic-slice_bitcast_fusion.1), dimensions={1,2} | broadcast | bytes 294912 | tf_op jit(solution)/shard_map/broadcast_in_dim | solution.py:492
  22.3 8.5 %all-to-all-start.1 = ((bf16[8,128,128]{2,1,0:T(8,128)(2,1)}), bf16[8,128,128]{2,1,0:T(8,128)(2,1)S(1)}, u32[]{:S(2)}, u32[]{:S(2)}) async-start(bf16[8,128,128]{2,1,0:T(8,128)(2,1)} %broadcast_in_dim.14), calls=%async_computation.1 | async-start | bytes 524288 | tf_op jit(solution)/shard_map/all_to_all | solution.py:493
  30.7 0.0 collective-permute-done.2.own_ref
  30.8 1.1 %collective-permute-start.3 = (bf16[16,128,128]{2,1,0:T(8,128)(2,1)S(1)}, bf16[16,128,128]{2,1,0:T(8,128)(2,1)S(1)}, u32[]{:S(2)}, u32[]{:S(2)}) collective-permute-start(bf16[16,128,128]{2,1,0:T(8,128)(2,1)S(1)} %collective-permute-done.2.own_ref), channel_id=1, source_target_pairs={{0,1},{1,0},{2,3},{3,2},{4,5},{5,4},{6,7},{7,6},{8,9},{9,8},{10,11... | collective-permute-start | bytes 1572872 | tf_op jit(solution)/shard_map/ppermute | solution.py:488
  31.8 3.0 %collective-permute-start = (s32[1]{0:T(128)}, s32[1]{0:T(128)}, u32[]{:S(2)}, u32[]{:S(2)}) collective-permute-start(s32[1]{0:T(128)} %bitcast.1), channel_id=1, source_target_pairs={{0,2},{2,0},{1,3},{3,1},{4,6},{6,4},{5,7},{7,5},{8,10},{10,8},{9,1... | collective-permute-start | bytes 20 | tf_op jit(solution)/shard_map/ppermute | solution.py:488
  35.5 5.7 %all-to-all-done.1 = bf16[8,128,128]{2,1,0:T(8,128)(2,1)S(1)} async-done(((bf16[8,128,128]{2,1,0:T(8,128)(2,1)}), bf16[8,128,128]{2,1,0:T(8,128)(2,1)S(1)}, u32[]{:S(2)}, u32[]{:S(2)}) %all-to-all-start.1) | async-done | bytes 262176 | tf_op jit(solution)/shard_map/all_to_all | solution.py:493
  41.2 0.0 copy-start.1
  41.2 0.0 copy-start.2
  41.2 2.5 %collective-permute-start.1 = (bf16[128,128]{1,0:T(8,128)(2,1)S(1)}, bf16[128,128]{1,0:T(8,128)(2,1)S(1)}, u32[]{:S(2)}, u32[]{:S(2)}) collective-permute-start(bf16[128,128]{1,0:T(8,128)(2,1)S(1)} %dynamic-slice_bitcast_fusion.own_ref), channel_id=1, source_target_pairs={{0,1},{1,0},{2,3},{3,2},{4,5},{5,4},{6,7},{7,6},{8,9},{9,8},{10,11... | collective-permute-start | bytes 98312 | tf_op jit(solution)/shard_map/ppermute | solution.py:488
  43.7 0.0 collective-permute-done.3.other_ref
  43.7 0.0 copy-done
  43.7 3.2 %factor.1 = (f32[16,128,128]{2,1,0:T(8,128)S(1)}, bf16[16,128,128]{2,1,0:T(8,128)(2,1)S(1)}) custom-call(s32[1]{0:T(128)} %bitcast.core_ref, bf16[16,128,128]{2,1,0:T(8,128)(2,1)S(1)} %copy-done, bf16[16,128,128]{2,1,0:T(8,128)(2,1)S(1)} %collective-permute-done.2.own_ref, bf16[16,128,128]{2,1,0:T(8,128)(2,1)S(1)} %collective-permute-done.3.other_ref), custom_call_target="tpu_custom_call" | custom-call | flops 4000000000 | bytes 6000000 | tf_op jit(solution)/shard_map/factor/pallas_call | solution.py:256
  46.9 0.0 copy-done.1
  46.9 0.0 copy-done.2
  46.9 0.0 copy-start.3
  46.9 0.0 copy-start.4
  47.0 3.3 %spectrum.1.spec_ref = bf16[13,256,256]{2,1,0:T(8,128)(2,1)S(1)} custom-call(s32[1]{0:T(128)} %bitcast.core_ref, bf16[16,128,128]{2,1,0:T(8,128)(2,1)S(1)} %get-tuple-element.7.tomo_ref, bf16[16,128,128]{2,1,0:T(8,128)(2,1)S(1)} %collective-permute-done.2.own_ref, bf16[16,128,128]{2,1,0:T(8,128)(2,1)S(1)} %collective-permute-done.3.other_ref, ...), custom_call_target="tpu_custom_call" | custom-call | flops 4000000000 | bytes 6000000 | tf_op jit(solution)/shard_map/spectrum/pallas_call | solution.py:277
  50.3 0.0 collective-permute-done.across_ref
  50.3 0.0 collective-permute-done.1.other_ref
  50.3 0.0 copy-done.3
  50.3 0.0 copy-done.4
  50.3 0.0 copy-start.5
  50.3 7.7 %match.1 = bf16[16,128,128]{2,1,0:T(8,128)(2,1)S(1)} custom-call(s32[1]{0:T(128)} %bitcast.core_ref, s32[1]{0:T(128)} %bitcast.10.orient_ref, s32[1]{0:T(128)} %collective-permute-done.across_ref, bf16[128,128]{1,0:T(8,128)(2,1)S(1)} %dynamic-slice_bitcast_fusion.own_ref, bf16[128,128]{1,0:T(8,128)(2,1)S(1)} %collective-permute-done.1.other_ref, ...), custom_call_target="tpu_custom_call" | custom-call | flops 8000000000 | bytes 6000000 | tf_op jit(solution)/shard_map/match/pallas_call | solution.py:465
  58.0 0.1 collective-permute-start.4
  58.1 0.0 copy-done.5
  58.1 1.9 %collective-permute-done.4 = bf16[16,128,128]{2,1,0:T(8,128)(2,1)S(1)} collective-permute-done((bf16[16,128,128]{2,1,0:T(8,128)(2,1)S(1)}, bf16[16,128,128]{2,1,0:T(8,128)(2,1)S(1)}, u32[]{:S(2)}, u32[]{:S(2)}) %collective-permute-start.4) | collective-permute-done | bytes 524320 | tf_op jit(solution)/shard_map/ppermute | solution.py:488
  60.0 1.1 %convert_multiply_fusion = f32[16,128,128]{2,1,0:T(8,128)} fusion(f32[16]{0:T(128)S(1)} %convert_element_type.23, bf16[16,128,128]{2,1,0:T(8,128)(2,1)S(1)} %match.1, bf16[16,128,128]{2,1,0:T(8,128)(2,1)S(1)} %collective-permute-done.4), kind=kLoop, calls=%fused_computation | loop fusion | flops 786432 | bytes 2097216 | tf_op jit(solution)/shard_map/mul | solution.py:529
  (3 shorter events, 0.0 us)
Async XLA Ops:
  0.0 43.7 %copy-start = (bf16[16,128,128]{2,1,0:T(8,128)(2,1)S(1)}, bf16[16,128,128]{2,1,0:T(8,128)(2,1)}, u32[]{:S(2)}) copy-start(bf16[16,128,128]{2,1,0:T(8,128)(2,1)} %tomo_hbm.1) | copy-start | bytes 1572868
  0.0 30.7 %collective-permute-start.2 = (bf16[16,128,128]{2,1,0:T(8,128)(2,1)}, bf16[16,128,128]{2,1,0:T(8,128)(2,1)S(1)}, u32[]{:S(2)}, u32[]{:S(2)}) collective-permute-start(bf16[16,128,128]{2,1,0:T(8,128)(2,1)} %tomo_hbm.1), channel_id=1, source_target_pairs={{4,0},{8,4},{9,1},{12,8},{13,5},{16,12},{17,9},{20,16},{21,13},{24... | collective-permute-start | bytes 1572872 | tf_op jit(solution)/shard_map/ppermute | solution.py:517
  3.1 18.4 %all-to-all-start = ((bf16[8,128,128]{2,1,0:T(8,128)(2,1)}), bf16[8,128,128]{2,1,0:T(8,128)(2,1)S(1)}, u32[]{:S(2)}, u32[]{:S(2)}) async-start(bf16[8,128,128]{2,1,0:T(8,128)(2,1)} %prep.1), calls=%async_computation | async-start | bytes 524288 | tf_op jit(solution)/shard_map/all_to_all | solution.py:514
  22.3 18.9 %all-to-all-start.1 = ((bf16[8,128,128]{2,1,0:T(8,128)(2,1)}), bf16[8,128,128]{2,1,0:T(8,128)(2,1)S(1)}, u32[]{:S(2)}, u32[]{:S(2)}) async-start(bf16[8,128,128]{2,1,0:T(8,128)(2,1)} %broadcast_in_dim.14), calls=%async_computation.1 | async-start | bytes 524288 | tf_op jit(solution)/shard_map/all_to_all | solution.py:493
  30.8 12.9 %collective-permute-start.3 = (bf16[16,128,128]{2,1,0:T(8,128)(2,1)S(1)}, bf16[16,128,128]{2,1,0:T(8,128)(2,1)S(1)}, u32[]{:S(2)}, u32[]{:S(2)}) collective-permute-start(bf16[16,128,128]{2,1,0:T(8,128)(2,1)S(1)} %collective-permute-done.2.own_ref), channel_id=1, source_target_pairs={{0,1},{1,0},{2,3},{3,2},{4,5},{5,4},{6,7},{7,6},{8,9},{9,8},{10,11... | collective-permute-start | bytes 1572872 | tf_op jit(solution)/shard_map/ppermute | solution.py:488
  31.8 18.4 %collective-permute-start = (s32[1]{0:T(128)}, s32[1]{0:T(128)}, u32[]{:S(2)}, u32[]{:S(2)}) collective-permute-start(s32[1]{0:T(128)} %bitcast.1), channel_id=1, source_target_pairs={{0,2},{2,0},{1,3},{3,1},{4,6},{6,4},{5,7},{7,5},{8,10},{10,8},{9,1... | collective-permute-start | bytes 20 | tf_op jit(solution)/shard_map/ppermute | solution.py:488
  41.2 5.7 %copy-start.1 = (bf16[256,256]{1,0:T(8,128)(2,1)S(1)}, bf16[256,256]{1,0:T(8,128)(2,1)}, u32[]{:S(2)}) copy-start(bf16[256,256]{1,0:T(8,128)(2,1)} %constant.35.first_ref) | copy-start | bytes 393220
  41.2 5.7 %copy-start.2 = (bf16[256,256]{1,0:T(8,128)(2,1)S(1)}, bf16[256,256]{1,0:T(8,128)(2,1)}, u32[]{:S(2)}) copy-start(bf16[256,256]{1,0:T(8,128)(2,1)} %constant.36.second_ref) | copy-start | bytes 393220
  41.2 9.1 %collective-permute-start.1 = (bf16[128,128]{1,0:T(8,128)(2,1)S(1)}, bf16[128,128]{1,0:T(8,128)(2,1)S(1)}, u32[]{:S(2)}, u32[]{:S(2)}) collective-permute-start(bf16[128,128]{1,0:T(8,128)(2,1)S(1)} %dynamic-slice_bitcast_fusion.own_ref), channel_id=1, source_target_pairs={{0,1},{1,0},{2,3},{3,2},{4,5},{5,4},{6,7},{7,6},{8,9},{9,8},{10,11... | collective-permute-start | bytes 98312 | tf_op jit(solution)/shard_map/ppermute | solution.py:488
  46.9 3.4 %copy-start.3 = (bf16[2,256,64]{2,1,0:T(8,128)(2,1)S(1)}, bf16[2,256,64]{2,1,0:T(8,128)(2,1)}, u32[]{:S(2)}) copy-start(bf16[2,256,64]{2,1,0:T(8,128)(2,1)} %constant.38.small_y_ref) | copy-start | bytes 196612
  46.9 3.4 %copy-start.4 = (bf16[2,64,256]{2,1,0:T(8,128)(2,1)S(1)}, bf16[2,64,256]{2,1,0:T(8,128)(2,1)}, u32[]{:S(2)}) copy-start(bf16[2,64,256]{2,1,0:T(8,128)(2,1)} %constant.37.small_z_ref) | copy-start | bytes 196612
  50.3 7.8 %copy-start.5 = (s32[16]{0:T(128)S(1)}, s32[16]{0:T(128)}, u32[]{:S(2)}) copy-start(s32[16]{0:T(128)} %param.13) | copy-start | bytes 196
  58.0 2.0 %collective-permute-start.4 = (bf16[16,128,128]{2,1,0:T(8,128)(2,1)S(1)}, bf16[16,128,128]{2,1,0:T(8,128)(2,1)S(1)}, u32[]{:S(2)}, u32[]{:S(2)}) collective-permute-start(bf16[16,128,128]{2,1,0:T(8,128)(2,1)S(1)} %match.1), channel_id=1, source_target_pairs={{0,1},{1,0},{2,3},{3,2},{4,5},{5,4},{6,7},{7,6},{8,9},{9,8},{10,11... | collective-permute-start | bytes 1572872 | tf_op jit(solution)/shard_map/ppermute | solution.py:488

commit v2 on v1

--- a/solution.py
+++ b/solution.py
@@ -12,6 +12,8 @@
 
 TILE = ("tile_0", "tile_1", "tile_2")
 EDGE = 32
+QUARTER = 64
+TAIL = 16
 SLAB = 16
 WIDE = 128
 LENGTH = 48
@@ -182,7 +184,8 @@
         run(two, one)
 
 
-def factor_kernel(core_ref, tomo_hbm, own_ref, other_ref, factor_ref, tomo_ref, sum_ref, square_ref, tomo_sem):
+def factor_kernel(core_ref, tomo_hbm, own_ref, other_ref, factor_hbm, tomo_ref,
+                  factor_ref, sum_ref, square_ref, tomo_sem, out_sems):
     fetch = pltpu.make_async_copy(tomo_hbm, tomo_ref, tomo_sem)
     fetch.start()
     volume = float(EDGE**3)
@@ -219,7 +222,14 @@
         factor_ref[x] = root * jnp.float32(2.0 / (LENGTH * WIDE * WIDE))
         return carry
 
-    lax.fori_loop(0, SLAB, scale, 0, unroll=4)
+    writes = []
+    for part in range(SLAB // 4):
+        lax.fori_loop(4 * part, 4 * part + 4, scale, 0, unroll=4)
+        at = pl.ds(4 * part, 4)
+        writes.append(pltpu.make_async_copy(factor_ref.at[at], factor_hbm.at[at], out_sems.at[part]))
+        writes[-1].start()
+    for write in writes:
+        write.wait()
 
 
 def spectrum_kernel(core_ref, tomo_ref, own_ref, other_ref, first_ref, second_ref, spec_ref, x_ref, z_ref):
@@ -253,18 +263,21 @@
 
 def factor_call(core, tomogram, own, other):
     vmem = pl.BlockSpec(memory_space=pltpu.VMEM)
+    hbm = pl.BlockSpec(memory_space=pltpu.HBM)
     return pl.pallas_call(
         factor_kernel,
         out_shape=(
             jax.ShapeDtypeStruct((SLAB, WIDE, WIDE), F32),
             jax.ShapeDtypeStruct((SLAB, WIDE, WIDE), BF16),
         ),
-        in_specs=[pl.BlockSpec(memory_space=pltpu.SMEM), pl.BlockSpec(memory_space=pl.ANY), vmem, vmem],
-        out_specs=(vmem, vmem),
+        in_specs=[pl.BlockSpec(memory_space=pltpu.SMEM), hbm, vmem, vmem],
+        out_specs=(hbm, vmem),
         scratch_shapes=[
             pltpu.VMEM((SLAB, WIDE, WIDE), F32),
             pltpu.VMEM((SLAB, WIDE, WIDE), F32),
+            pltpu.VMEM((SLAB, WIDE, WIDE), F32),
             pltpu.SemaphoreType.DMA,
+            pltpu.SemaphoreType.DMA((SLAB // 4,)),
         ],
         compiler_params=pltpu.CompilerParams(vmem_limit_bytes=8 << 20),
         cost_estimate=pl.CostEstimate(flops=4_000_000_000, transcendentals=0, bytes_accessed=6_000_000),
@@ -289,28 +302,32 @@
     )(core, tomogram, own, other, first, second)
 
 
-def prep_kernel(core_ref, temp_ref, packed_ref):
+def prep_kernel(core_ref, far_ref, orient_ref, temp_ref, packed_ref):
     values = temp_ref[0].astype(F32).reshape(SLAB * EDGE, EDGE)
     rows = 4 * EDGE
-    packed = jnp.concatenate([values[g * rows:(g + 1) * rows] for g in range(4)], axis=1).astype(BF16)
+    packed = jnp.concatenate([values[g * rows:(g + 1) * rows] for g in range(4)], axis=1)
+    packed = jnp.where(far_ref[0] == 0, packed[:QUARTER], packed[QUARTER:]).astype(BF16)
+    index = jnp.full((TAIL, WIDE), orient_ref[0], jnp.int32).astype(F32).astype(BF16)
     for member in range(packed_ref.shape[0]):
-        packed_ref[member] = packed
-
-
-def prep_call(core, templates, members):
+        packed_ref[member, :QUARTER] = packed
+        packed_ref[member, QUARTER:] = index
+
+
+def prep_call(core, far, orient, templates, members):
+    shape = (members, QUARTER + TAIL, WIDE)
     return pl.pallas_call(
         prep_kernel,
-        out_shape=jax.ShapeDtypeStruct((members, WIDE, WIDE), BF16),
+        out_shape=jax.ShapeDtypeStruct(shape, BF16),
         grid_spec=pltpu.PrefetchScalarGridSpec(
-            num_scalar_prefetch=1,
+            num_scalar_prefetch=3,
             grid=(1,),
             in_specs=[
-                pl.BlockSpec((1, EDGE // 2, EDGE, EDGE), lambda i, core: (0, core[0], 0, 0)),
+                pl.BlockSpec((1, EDGE // 2, EDGE, EDGE), lambda i, core, far, orient: (0, core[0], 0, 0)),
             ],
-            out_specs=pl.BlockSpec((members, WIDE, WIDE), lambda i, core: (0, 0, 0)),
+            out_specs=pl.BlockSpec(shape, lambda i, core, far, orient: (0, 0, 0)),
         ),
         name="prep",
-    )(core, templates)
+    )(core, far, orient, templates)
 
 
 def turns_of(index):
@@ -348,11 +365,17 @@
         source = target
 
 
-def match_kernel(core_ref, orient_ref, across_ref, own_ref, other_ref, spec_ref, factor_ref, first_ref, second_ref,
+def match_kernel(core_ref, own_ref, other_ref, spec_ref, factor_hbm, first_ref, second_ref,
                  small_z_ref, small_y_ref, best_ref,
-                 base_ref, cube_ref, spare_ref, packed_ref, a_ref, z_ref, p_ref, q_ref, f_ref):
+                 factor_ref, base_ref, cube_ref, spare_ref, packed_ref, a_ref, z_ref, p_ref, q_ref, f_ref,
+                 factor_sem):
     core = core_ref[0]
-    halves = [ref[...].astype(F32) for ref in (own_ref, other_ref)]
+    fetch = pltpu.make_async_copy(factor_hbm, factor_ref, factor_sem)
+    fetch.start()
+    halves = [
+        jnp.concatenate([ref[0, :QUARTER], ref[1, :QUARTER]], axis=0).astype(F32) for ref in (own_ref, other_ref)
+    ]
+    orients = [jnp.max(own_ref[o, QUARTER:].astype(F32)).astype(jnp.int32) for o in range(2)]
     total = float(EDGE**3)
     center = jnp.sum(halves[0] + halves[1]) / total
     halves = [half - center for half in halves]
@@ -365,7 +388,7 @@
             base_ref[pl.ds(start, 4 * EDGE), :] = half[:, group * EDGE:(group + 1) * EDGE]
 
     flips = []
-    for o, index in enumerate((orient_ref[0], across_ref[0])):
+    for o, index in enumerate(orients):
         turns, flipped = turns_of(index)
         flips.append(flipped)
         turn(base_ref, cube_ref.at[o], spare_ref.at[o], turns)
@@ -455,19 +478,22 @@
             best_ref[x, pl.ds(at, 16), :] = value.astype(BF16)
         return carry
 
+    fetch.wait()
     lax.fori_loop(0, WIDE // 16, scores, 0)
 
 
-def match_call(core, orient, across, own, other, spec, factor, first, second, small_z, small_y):
+def match_call(core, own, other, spec, factor, first, second, small_z, small_y):
     vmem = pl.BlockSpec(memory_space=pltpu.VMEM)
     smem = pl.BlockSpec(memory_space=pltpu.SMEM)
+    hbm = pl.BlockSpec(memory_space=pltpu.HBM)
     cube = EDGE * EDGE
     return pl.pallas_call(
         match_kernel,
         out_shape=jax.ShapeDtypeStruct((SLAB, WIDE, WIDE), BF16),
-        in_specs=[smem] * 3 + [vmem] * 8,
+        in_specs=[smem, vmem, vmem, vmem, hbm] + [vmem] * 4,
         out_specs=vmem,
         scratch_shapes=[
+            pltpu.VMEM((SLAB, WIDE, WIDE), F32),
             pltpu.VMEM((cube, EDGE), F32),
             pltpu.VMEM((2, cube, EDGE), F32),
             pltpu.VMEM((2, cube, EDGE), F32),
@@ -477,21 +503,16 @@
             pltpu.VMEM((2, FREQS, WIDE, 2 * WIDE), BF16),
             pltpu.VMEM((2, PAIRS, 2 * WIDE, 2 * WIDE), BF16),
             pltpu.VMEM((2, PAIRS, 2 * WIDE, 2 * WIDE), F32),
+            pltpu.SemaphoreType.DMA,
         ],
         compiler_params=pltpu.CompilerParams(vmem_limit_bytes=24 << 20),
         cost_estimate=pl.CostEstimate(flops=8_000_000_000, transcendentals=0, bytes_accessed=6_000_000),
         name="match",
-    )(core, orient, across, own, other, spec, factor, first, second, small_z, small_y)
+    )(core, own, other, spec, factor, first, second, small_z, small_y)
 
 
 def swapped(value, axis):
     return lax.ppermute(value, axis, [(0, 1), (1, 0)])
-
-
-def from_member(value, axis, root):
-    sent = jnp.broadcast_to(value[None], (lax.axis_size(axis), *value.shape))
-    got = lax.all_to_all(sent, axis, 0, 0, tiled=True)
-    return lax.dynamic_index_in_dim(got, root, 0, keepdims=False)
 
 
 def halo_pairs(tiles):
@@ -506,25 +527,28 @@
 def shards(tomogram, templates, owners, orient_ids, slice_mask):
     core_arg = lax.axis_index("core").astype(jnp.int32)[None]
     first, second, small_z, small_y = tables()
-    columns = lax.axis_size("tile_2")
-    depth, plane = lax.axis_size("tile_0"), lax.axis_size("tile_1") * columns
+    far_arg = lax.axis_index("far").astype(jnp.int32)[None]
+    depth, plane = lax.axis_size("tile_0"), lax.axis_size(("tile_1", "tile_2"))
     root_plane, root_z = lax.rem(owners[0], plane), lax.div(owners[0], plane)
 
-    sent = prep_call(core_arg, templates, plane)
-    got = lax.all_to_all(sent, ("tile_1", "tile_2"), 0, 0, tiled=True)
-    half = lax.dynamic_index_in_dim(got, root_plane, 0, keepdims=False)
+    sent = prep_call(core_arg, far_arg, orient_ids[0], templates, depth)
+    got = lax.all_to_all(sent, "tile_0", 0, 0, tiled=True)
+    part = lax.dynamic_index_in_dim(got, root_z, 0, keepdims=False)
 
     halo = lax.ppermute(tomogram, TILE + ("core",), halo_pairs(depth * plane))
-    across = swapped(orient_ids[0], "far")
     other_halo = swapped(halo, "core")
 
-    half = from_member(half, "tile_0", root_z)
-    other_half = swapped(half, "core")
+    sent = jnp.broadcast_to(part[None], (2 * plane, *part.shape))
+    got = lax.all_to_all(sent, ("tile_1", "tile_2", "far"), 0, 0, tiled=True)
+    quarters = lax.dynamic_slice_in_dim(got, 2 * root_plane, 2, 0)
+    other_quarters = swapped(quarters, "core")
 
     factor, staged = factor_call(core_arg, tomogram, halo, other_halo)
     spec = spectrum_call(core_arg, staged, halo, other_halo, first, second)
 
-    best = match_call(core_arg, orient_ids[0], across, half, other_half, spec, factor, first, second, small_z, small_y)
+    best = match_call(
+        core_arg, quarters, other_quarters, spec, factor, first, second, small_z, small_y
+    )
     best = jnp.maximum(best, swapped(best, "core"))
     return best.astype(F32) * slice_mask.astype(F32)[:, None, None]
 

time: 62.1 us -> 59 us (0.950); the launches traced: 61.2 us -> 58.7 us
  waiting for transfers between devices: 18.4 us -> 15 us
  starting transfers between devices: 23.4 us -> 24.7 us
    all_to_all x2, waiting for transfers between devices: 16.6 us -> 13.1 us  [the longest x1 7.61 us: shards(): got = lax.all_to_all(sent, ('tile_1', 'tile_2', 'far'), 0, 0, tiled=True)]
    all_to_all x2, starting transfers between devices: 15.3 us -> 17.4 us  [the longest x1 12.4 us: shards(): got = lax.all_to_all(sent, 'tile_0', 0, 0, tiled=True)]
    ppermute x4 -> x3, starting transfers between devices: 6.64 us -> 5.96 us  [swapped(): return lax.ppermute(value, axis, [(0, 1), (1, 0)])]
    ppermute x4 -> x3, waiting for transfers between devices: 1.88 us -> 1.88 us  [swapped(): return lax.ppermute(value, axis, [(0, 1), (1, 0)])]
  transfers between devices with their start and end apart: 7 -> 6, of which waited for: 3 -> 3; matrix products, arithmetic and copies ran while one was open for 1% -> 1% of each run, Pallas kernels for 13% -> 14%
where the time goes in v2:
time: 59 us; the launch traced here: 58.7 us
  starting transfers between devices  24.7 us (42%)
  Pallas kernels  15.6 us (26%)
  waiting for transfers between devices  15 us (25%)
  between operations  1.47 us (2%)
  other arithmetic  1.14 us (2%)
  local copies, waits for them, and re-layouts  0.81 us (1%)
    all_to_all x1, starting transfers between devices, shards(): got = lax.all_to_all(sent, 'tile_0', 0, 0, tiled=True)  12.4 us
    all_to_all x1, waiting for transfers between devices, shards(): got = lax.all_to_all(sent, ('tile_1', 'tile_2', 'far'), 0, 0, tiled=True)  7.61 us
    pallas_call x1, Pallas kernels, match_call(): pl.pallas_call(match_kernel, out_shape=jax.ShapeDtypeStruct((SLAB, WIDE,...  7.3 us
    ppermute x3, starting transfers between devices, swapped(): return lax.ppermute(value, axis, [(0, 1), (1, 0)])  5.96 us
    all_to_all x1, waiting for transfers between devices, shards(): got = lax.all_to_all(sent, 'tile_0', 0, 0, tiled=True)  5.46 us
    all_to_all x1, starting transfers between devices, shards(): got = lax.all_to_all(sent, ('tile_1', 'tile_2', 'far'), 0, 0, tiled=True)  5.02 us
    pallas_call x1, Pallas kernels, spectrum_call(): pl.pallas_call(spectrum_kernel, out_shape=jax.ShapeDtypeStruct((PAIRS, 2...  3.33 us
    pallas_call x1, Pallas kernels, factor_call(): pl.pallas_call(factor_kernel, out_shape=(jax.ShapeDtypeStruct((SLAB, WIDE...  3.29 us
  transfers between devices with their start and end apart: 6, of which 3 were waited for; matrix products, arithmetic and copies ran while one was open for 1% of the time, Pallas kernels for 14%

profile of v2, /device:TPU:1, one launch (start us, length us, event | category | flops | bytes accessed | tf_op | source)
XLA Modules:
  0.0 58.7 jit_solution(99832398835028506)
XLA Ops:
  0.0 0.0 copy-start
  0.0 1.4 %collective-permute-start.1 = (bf16[16,128,128]{2,1,0:T(8,128)(2,1)}, bf16[16,128,128]{2,1,0:T(8,128)(2,1)S(1)}, u32[]{:S(2)}, u32[]{:S(2)}) collective-permute-start(bf16[16,128,128]{2,1,0:T(8,128)(2,1)} %tomo_hbm.1), channel_id=1, source_target_pairs={{4,0},{8,4},{9,1},{12,8},{13,5},{16,12},{17,9},{20,16},{21,13},{24... | collective-permute-start | bytes 1572872 | tf_op jit(solution)/shard_map/ppermute | solution.py:538
  2.1 1.7 %prep.1 = bf16[8,80,128]{2,1,0:T(8,128)(2,1)} custom-call(s32[1]{0:T(128)} %bitcast.core_ref, s32[1]{0:T(128)} %bitcast.1.far_ref, s32[1]{0:T(128)} %bitcast.9.orient_ref, bf16[1,32,32,32]{3,2,1,0:T(8,128)(2,1)} %temp_ref.1), custom_call_target="tpu_custom_call" | custom-call | tf_op jit(solution)/shard_map/prep/pallas_call | solution.py:318
  3.7 12.4 %all-to-all-start = ((bf16[8,80,128]{2,1,0:T(8,128)(2,1)}), bf16[8,80,128]{2,1,0:T(8,128)(2,1)S(1)}, u32[]{:S(2)}, u32[]{:S(2)}) async-start(bf16[8,80,128]{2,1,0:T(8,128)(2,1)} %prep.1), calls=%async_computation | async-start | bytes 327680 | tf_op jit(solution)/shard_map/all_to_all | solution.py:535
  16.8 0.0 collective-permute-done.1.own_ref
  16.8 2.2 %collective-permute-start.2 = (bf16[16,128,128]{2,1,0:T(8,128)(2,1)S(1)}, bf16[16,128,128]{2,1,0:T(8,128)(2,1)S(1)}, u32[]{:S(2)}, u32[]{:S(2)}) collective-permute-start(bf16[16,128,128]{2,1,0:T(8,128)(2,1)S(1)} %collective-permute-done.1.own_ref), channel_id=1, source_target_pairs={{0,1},{1,0},{2,3},{3,2},{4,5},{5,4},{6,7},{7,6},{8,9},{9,8},{10,11... | collective-permute-start | bytes 1572872 | tf_op jit(solution)/shard_map/ppermute | solution.py:515
  19.0 5.5 %all-to-all-done = bf16[8,80,128]{2,1,0:T(8,128)(2,1)S(1)} async-done(((bf16[8,80,128]{2,1,0:T(8,128)(2,1)}), bf16[8,80,128]{2,1,0:T(8,128)(2,1)S(1)}, u32[]{:S(2)}, u32[]{:S(2)}) %all-to-all-start) | async-done | bytes 163872 | tf_op jit(solution)/shard_map/all_to_all | solution.py:535
  24.5 0.8 %broadcast_in_dim.18 = bf16[16,80,128]{2,1,0:T(8,128)(2,1)} broadcast(bf16[80,128]{1,0:T(8,128)(2,1)S(1)} %dynamic-slice_bitcast_fusion), dimensions={1,2} | broadcast | bytes 348160 | tf_op jit(solution)/shard_map/broadcast_in_dim | solution.py:541
  25.3 5.0 %all-to-all-start.1 = ((bf16[16,80,128]{2,1,0:T(8,128)(2,1)}), bf16[16,80,128]{2,1,0:T(8,128)(2,1)S(1)}, u32[]{:S(2)}, u32[]{:S(2)}) async-start(bf16[16,80,128]{2,1,0:T(8,128)(2,1)} %broadcast_in_dim.18), calls=%async_computation.1 | async-start | bytes 655360 | tf_op jit(solution)/shard_map/all_to_all | solution.py:542
  30.3 7.6 %all-to-all-done.1 = bf16[16,80,128]{2,1,0:T(8,128)(2,1)S(1)} async-done(((bf16[16,80,128]{2,1,0:T(8,128)(2,1)}), bf16[16,80,128]{2,1,0:T(8,128)(2,1)S(1)}, u32[]{:S(2)}, u32[]{:S(2)}) %all-to-all-start.1) | async-done | bytes 327712 | tf_op jit(solution)/shard_map/all_to_all | solution.py:542
  37.9 0.0 copy-start.1
  37.9 0.0 copy-start.2
  37.9 3.6 %collective-permute-start = (bf16[2,80,128]{2,1,0:T(8,128)(2,1)S(1)}, bf16[2,80,128]{2,1,0:T(8,128)(2,1)S(1)}, u32[]{:S(2)}, u32[]{:S(2)}) collective-permute-start(bf16[2,80,128]{2,1,0:T(8,128)(2,1)S(1)} %constant_dynamic-slice_fusion.own_ref), channel_id=1, source_target_pairs={{0,1},{1,0},{2,3},{3,2},{4,5},{5,4},{6,7},{7,6},{8,9},{9,8},{10,11... | collective-permute-start | bytes 122888 | tf_op jit(solution)/shard_map/ppermute | solution.py:515
  41.5 0.0 collective-permute-done.2.other_ref
  41.5 0.0 copy-done
  41.5 3.3 %factor.1 = (f32[16,128,128]{2,1,0:T(8,128)S(1)}, bf16[16,128,128]{2,1,0:T(8,128)(2,1)S(1)}) custom-call(s32[1]{0:T(128)} %bitcast.core_ref, bf16[16,128,128]{2,1,0:T(8,128)(2,1)S(1)} %copy-done, bf16[16,128,128]{2,1,0:T(8,128)(2,1)S(1)} %collective-permute-done.1.own_ref, bf16[16,128,128]{2,1,0:T(8,128)(2,1)S(1)} %collective-permute-done.2.other_ref), custom_call_target="tpu_custom_call" | custom-call | flops 4000000000 | bytes 6000000 | tf_op jit(solution)/shard_map/factor/pallas_call | solution.py:267
  44.8 0.0 copy-done.1
  44.9 0.0 copy-done.2
  44.9 0.0 copy-start.3
  44.9 0.0 copy-start.4
  44.9 3.3 %spectrum.1.spec_ref = bf16[13,256,256]{2,1,0:T(8,128)(2,1)S(1)} custom-call(s32[1]{0:T(128)} %bitcast.core_ref, bf16[16,128,128]{2,1,0:T(8,128)(2,1)S(1)} %get-tuple-element.7.tomo_ref, bf16[16,128,128]{2,1,0:T(8,128)(2,1)S(1)} %collective-permute-done.1.own_ref, bf16[16,128,128]{2,1,0:T(8,128)(2,1)S(1)} %collective-permute-done.2.other_ref, ...), custom_call_target="tpu_custom_call" | custom-call | flops 4000000000 | bytes 6000000 | tf_op jit(solution)/shard_map/spectrum/pallas_call | solution.py:290
  48.2 0.0 collective-permute-done.other_ref
  48.2 0.0 copy-done.3
  48.2 0.0 copy-done.4
  48.3 0.0 copy-start.5
  48.3 7.3 %match.1 = bf16[16,128,128]{2,1,0:T(8,128)(2,1)S(1)} custom-call(s32[1]{0:T(128)} %bitcast.core_ref, bf16[2,80,128]{2,1,0:T(8,128)(2,1)S(1)} %constant_dynamic-slice_fusion.own_ref, bf16[2,80,128]{2,1,0:T(8,128)(2,1)S(1)} %collective-permute-done.other_ref, bf16[13,256,256]{2,1,0:T(8,128)(2,1)S(1)} %spectrum.1.spec_ref, ...), custom_call_target="tpu_custom_call" | custom-call | flops 8000000000 | bytes 6000000 | tf_op jit(solution)/shard_map/match/pallas_call | solution.py:490
  55.6 0.1 collective-permute-start.3
  55.7 0.0 copy-done.5
  55.7 1.9 %collective-permute-done.3 = bf16[16,128,128]{2,1,0:T(8,128)(2,1)S(1)} collective-permute-done((bf16[16,128,128]{2,1,0:T(8,128)(2,1)S(1)}, bf16[16,128,128]{2,1,0:T(8,128)(2,1)S(1)}, u32[]{:S(2)}, u32[]{:S(2)}) %collective-permute-start.3) | collective-permute-done | bytes 524320 | tf_op jit(solution)/shard_map/ppermute | solution.py:515
  57.6 1.1 %convert_multiply_fusion = f32[16,128,128]{2,1,0:T(8,128)} fusion(f32[16]{0:T(128)S(1)} %convert_element_type.23, bf16[16,128,128]{2,1,0:T(8,128)(2,1)S(1)} %match.1, bf16[16,128,128]{2,1,0:T(8,128)(2,1)S(1)} %collective-permute-done.3), kind=kLoop, calls=%fused_computation | loop fusion | flops 786432 | bytes 2097216 | tf_op jit(solution)/shard_map/mul | solution.py:553
  (3 shorter events, 0.0 us)
Async XLA Ops:
  0.0 41.5 %copy-start = (bf16[16,128,128]{2,1,0:T(8,128)(2,1)S(1)}, bf16[16,128,128]{2,1,0:T(8,128)(2,1)}, u32[]{:S(2)}) copy-start(bf16[16,128,128]{2,1,0:T(8,128)(2,1)} %tomo_hbm.1) | copy-start | bytes 1572868
  0.0 16.8 %collective-permute-start.1 = (bf16[16,128,128]{2,1,0:T(8,128)(2,1)}, bf16[16,128,128]{2,1,0:T(8,128)(2,1)S(1)}, u32[]{:S(2)}, u32[]{:S(2)}) collective-permute-start(bf16[16,128,128]{2,1,0:T(8,128)(2,1)} %tomo_hbm.1), channel_id=1, source_target_pairs={{4,0},{8,4},{9,1},{12,8},{13,5},{16,12},{17,9},{20,16},{21,13},{24... | collective-permute-start | bytes 1572872 | tf_op jit(solution)/shard_map/ppermute | solution.py:538
  3.7 20.7 %all-to-all-start = ((bf16[8,80,128]{2,1,0:T(8,128)(2,1)}), bf16[8,80,128]{2,1,0:T(8,128)(2,1)S(1)}, u32[]{:S(2)}, u32[]{:S(2)}) async-start(bf16[8,80,128]{2,1,0:T(8,128)(2,1)} %prep.1), calls=%async_computation | async-start | bytes 327680 | tf_op jit(solution)/shard_map/all_to_all | solution.py:535
  16.8 24.8 %collective-permute-start.2 = (bf16[16,128,128]{2,1,0:T(8,128)(2,1)S(1)}, bf16[16,128,128]{2,1,0:T(8,128)(2,1)S(1)}, u32[]{:S(2)}, u32[]{:S(2)}) collective-permute-start(bf16[16,128,128]{2,1,0:T(8,128)(2,1)S(1)} %collective-permute-done.1.own_ref), channel_id=1, source_target_pairs={{0,1},{1,0},{2,3},{3,2},{4,5},{5,4},{6,7},{7,6},{8,9},{9,8},{10,11... | collective-permute-start | bytes 1572872 | tf_op jit(solution)/shard_map/ppermute | solution.py:515
  25.3 12.7 %all-to-all-start.1 = ((bf16[16,80,128]{2,1,0:T(8,128)(2,1)}), bf16[16,80,128]{2,1,0:T(8,128)(2,1)S(1)}, u32[]{:S(2)}, u32[]{:S(2)}) async-start(bf16[16,80,128]{2,1,0:T(8,128)(2,1)} %broadcast_in_dim.18), calls=%async_computation.1 | async-start | bytes 655360 | tf_op jit(solution)/shard_map/all_to_all | solution.py:542
  37.9 6.9 %copy-start.1 = (bf16[256,256]{1,0:T(8,128)(2,1)S(1)}, bf16[256,256]{1,0:T(8,128)(2,1)}, u32[]{:S(2)}) copy-start(bf16[256,256]{1,0:T(8,128)(2,1)} %constant.40.first_ref) | copy-start | bytes 393220
  37.9 6.9 %copy-start.2 = (bf16[256,256]{1,0:T(8,128)(2,1)S(1)}, bf16[256,256]{1,0:T(8,128)(2,1)}, u32[]{:S(2)}) copy-start(bf16[256,256]{1,0:T(8,128)(2,1)} %constant.41.second_ref) | copy-start | bytes 393220
  37.9 10.3 %collective-permute-start = (bf16[2,80,128]{2,1,0:T(8,128)(2,1)S(1)}, bf16[2,80,128]{2,1,0:T(8,128)(2,1)S(1)}, u32[]{:S(2)}, u32[]{:S(2)}) collective-permute-start(bf16[2,80,128]{2,1,0:T(8,128)(2,1)S(1)} %constant_dynamic-slice_fusion.own_ref), channel_id=1, source_target_pairs={{0,1},{1,0},{2,3},{3,2},{4,5},{5,4},{6,7},{7,6},{8,9},{9,8},{10,11... | collective-permute-start | bytes 122888 | tf_op jit(solution)/shard_map/ppermute | solution.py:515
  44.9 3.4 %copy-start.3 = (bf16[2,256,64]{2,1,0:T(8,128)(2,1)S(1)}, bf16[2,256,64]{2,1,0:T(8,128)(2,1)}, u32[]{:S(2)}) copy-start(bf16[2,256,64]{2,1,0:T(8,128)(2,1)} %constant.43.small_y_ref) | copy-start | bytes 196612
  44.9 3.4 %copy-start.4 = (bf16[2,64,256]{2,1,0:T(8,128)(2,1)S(1)}, bf16[2,64,256]{2,1,0:T(8,128)(2,1)}, u32[]{:S(2)}) copy-start(bf16[2,64,256]{2,1,0:T(8,128)(2,1)} %constant.42.small_z_ref) | copy-start | bytes 196612
  48.3 7.4 %copy-start.5 = (s32[16]{0:T(128)S(1)}, s32[16]{0:T(128)}, u32[]{:S(2)}) copy-start(s32[16]{0:T(128)} %param.13) | copy-start | bytes 196
  55.6 2.0 %collective-permute-start.3 = (bf16[16,128,128]{2,1,0:T(8,128)(2,1)S(1)}, bf16[16,128,128]{2,1,0:T(8,128)(2,1)S(1)}, u32[]{:S(2)}, u32[]{:S(2)}) collective-permute-start(bf16[16,128,128]{2,1,0:T(8,128)(2,1)S(1)} %match.1), channel_id=1, source_target_pairs={{0,1},{1,0},{2,3},{3,2},{4,5},{5,4},{6,7},{7,6},{8,9},{9,8},{10,11... | collective-permute-start | bytes 1572872 | tf_op jit(solution)/shard_map/ppermute | solution.py:515
